TPU v7x, 512 devices: a whole 4x8x8 slice. The times are simulated.
512 devices in a mesh: gy: 64 (over z, x, core), gz: 8 (over y).
Axes of the slice: x: 4, y: 8, z: 8, core: 2. Of those that a mesh axis runs over, the one named last changes fastest.
Arguments:
- velocity: float32 [3, 1536, 4096], P(None, ('gy', 'gz')), may hold values from -6 to 6
- explicit: float32 [3, 1536, 4096], P(None, ('gy', 'gz')), may hold values from -6 to 6
- bands: float32 [2, 5, 1536], P(None, None, 'gy'), may hold values from -0.6 to 0.6
- inverse: float32 [1536, 24, 2048], P('gy', None, 'gz'), may hold values from -1.25 to 1.25
- spikes: float32 [2, 2, 1536, 2048], P(None, None, 'gy', 'gz'), may hold values from -1.4 to 1.4
Outputs:
- updated: float32 [3, 1536, 4096], P(None, 'gy', 'gz')
All inputs are finite; a program needn't handle non-finite values.
Results may differ from a plain program's by a relative error of at most 0.00024.
Values sent between devices are 32-bit elements; how exact they have to be, the bound alone decides.
A program may use at most 64 MiB of HBM per device.

v0:
```python
import jax
import jax.numpy as jnp
from jax import lax
from jax.sharding import PartitionSpec as P


def cut_along(value, dim, peers):
    lengths = value.shape
    pieces = value.reshape(*lengths[:dim], peers, lengths[dim] // peers, *lengths[dim + 1 :])
    return jnp.moveaxis(pieces, dim, 0)


def cut_rows(length, count):
    unit = 8 if length >= 8 * count else 1
    return [length // unit * k // count * unit for k in range(1, count)]


def in_order(pieces, dim):
    pieces = jnp.moveaxis(pieces, 0, dim)
    lengths = pieces.shape
    return pieces.reshape(*lengths[:dim], lengths[dim] * lengths[dim + 1], *lengths[dim + 2 :])


def several_exchanges(value, axis, pieces, split_dim, concat_dim):
    blocks = cut_along(value, split_dim, lax.axis_size(axis))
    cut = max(range(1, max(2, blocks.ndim - 1)), key=lambda d: blocks.shape[d])
    finished = []
    for section in jnp.split(blocks, cut_rows(blocks.shape[cut], pieces), axis=cut):
        if section.size:
            finished.append(lax.all_to_all(section, axis, split_axis=0, concat_axis=0, tiled=True))
    return in_order(jnp.concatenate(finished, axis=cut), concat_dim)


def extended(cells, sides, width):
    for axis, dim in sides:
        count = lax.axis_size(axis)
        ends = count - 1
        head = lax.slice_in_dim(cells, 0, width, axis=dim)
        tail = lax.slice_in_dim(cells, cells.shape[dim] - width, cells.shape[dim], axis=dim)
        cells = jnp.concatenate(
            [
                lax.ppermute(tail, axis, [(i, (i + 1) % count) for i in range(ends)]),
                cells,
                lax.ppermute(head, axis, [((i + 1) % count, i) for i in range(ends)]),
            ],
            axis=dim,
        )
    return cells


def copy_for_each(value, axis):
    copies = jnp.broadcast_to(value, (lax.axis_size(axis), *value.shape))
    return lax.all_to_all(copies, axis, split_axis=0, concat_axis=0, tiled=True)


def gathered_once(value, axis):
    leaves = jax.tree.leaves(value)
    sequence = sorted(range(len(leaves)), key=lambda k: -leaves[k].size)
    width = (1, *leaves[sequence[0]].shape)[-1]
    lines = [
        jnp.pad(leaves[k].reshape(-1), (0, -leaves[k].size % width)).reshape(-1, width)
        for k in sequence
    ]
    both, at, found = (copy_for_each(jnp.concatenate(lines), axis), 0, {})
    for k, line in zip(sequence, lines):
        section = both[:, at : at + len(line)].reshape(len(both), -1)
        found[k] = section[:, : leaves[k].size].reshape(-1, *leaves[k].shape)
        at += len(line)
    numbers = iter(range(len(leaves)))
    return jax.tree.map(lambda _: found[next(numbers)], value)


def joined_by_halves(pieces, combine):
    while len(jax.tree.leaves(pieces)[0]) > 1:
        pieces = jax.vmap(combine)(
            *(jax.tree.map(lambda part: part[side::2], pieces) for side in (0, 1))
        )
    return jax.tree.map(lambda part: part[0], pieces)


def prefix_2(value, axis, combine, identity):
    peers, index = (lax.axis_size(axis), lax.axis_index(axis))
    passed = jnp.arange(peers) < index

    def prefix_kept(part, zero, own):
        part = jnp.where(
            passed.reshape(-1, *(1 for _ in own.shape)), part, jnp.asarray(zero, own.dtype)
        )
        return part

    pieces = gathered_once(value, axis)
    return joined_by_halves(jax.tree.map(prefix_kept, pieces, identity, value), combine)


def once_a_type(value, axis):
    leaves, found = (jax.tree.leaves(value), {})
    for first, a in enumerate(leaves):
        if first not in found:
            alike = [k for k, b in enumerate(leaves) if b.dtype == a.dtype]
            got = (
                gathered_once([leaves[k] for k in alike], axis)
                if len(alike) > 1
                else [copy_for_each(a, axis)]
            )
            for k, b in zip(alike, got):
                found[k] = b
    numbers = iter(range(len(leaves)))
    return jax.tree.map(lambda _: found[next(numbers)], value)


def carried_in(value, axis, combine, identity):
    peers, index = (lax.axis_size(axis), lax.axis_index(axis))
    passed = jnp.arange(peers) > index

    def carried_kept(part, zero, own):
        part = jnp.where(
            passed.reshape(-1, *(1 for _ in own.shape)), part, jnp.asarray(zero, own.dtype)
        )
        return part[::-1]

    pieces = once_a_type(value, axis)
    return joined_by_halves(jax.tree.map(carried_kept, pieces, identity, value), combine)


def couple(spike, state):
    first = spike[..., 0, :, :][..., None, :, :, None] * state[..., :, 0, :, :][..., :, None, :, :]
    second = spike[..., 1, :, :][..., None, :, :, None] * state[..., :, 1, :, :][..., :, None, :, :]
    return first + second


def apply_map(matrix, state):
    first = matrix[..., :, 0, :][..., None, :, :, None] * state[..., :, 0, :, :][..., :, None, :, :]
    second = (
        matrix[..., :, 1, :][..., None, :, :, None] * state[..., :, 1, :, :][..., :, None, :, :]
    )
    return first + second


def compose(later, earlier):
    first = later[..., :, 0, :][..., :, None, :] * earlier[..., 0, :, :][..., None, :, :]
    second = later[..., :, 1, :][..., :, None, :] * earlier[..., 1, :, :][..., None, :, :]
    return first + second


def combine(earlier, later):
    return (compose(later[0], earlier[0]), apply_map(later[0], earlier[1]) + later[1])


def per_device(velocity, explicit, bands, inverse, spikes):
    stacked = jnp.stack([velocity, velocity + explicit])
    moved = several_exchanges(stacked, "gz", 2, 3, 2)
    rows = moved.shape[2]
    modes = inverse.shape[2]
    padded = extended(moved, (("gy", 2),), 2)
    rhs = jnp.zeros(moved.shape[1:], jnp.float32)
    for offset in range(5):
        rhs = rhs + bands[0, offset][None, :, None] * padded[1][:, offset : offset + rows]
        rhs = rhs + bands[1, offset][None, :, None] * padded[0][:, offset : offset + rows]
    rhs_modes = rhs.reshape(3, rows, modes, 2)
    local = jnp.einsum("rcm,fcmp->frmp", inverse, rhs_modes, precision=lax.Precision.HIGHEST)
    lower = spikes[0]
    upper = spikes[1]
    down_map = -jnp.transpose(lower[:, rows - 2 :], (1, 0, 2))
    up_map = -jnp.transpose(upper[:, 0:2], (1, 0, 2))
    eye_map = jnp.broadcast_to(jnp.eye(2, dtype=jnp.float32)[:, :, None], (2, 2, modes))
    zero_state = jnp.zeros((3, 2, modes, 2), jnp.float32)
    prefix = prefix_2((down_map, local[:, rows - 2 :]), "gy", combine, (eye_map, zero_state))
    before = prefix[1]
    zvals = local - couple(lower, before)
    suffix = carried_in((up_map, zvals[:, 0:2]), "gy", combine, (eye_map, zero_state))
    after = suffix[1]
    result = zvals - couple(upper, after)
    return result.reshape(3, rows, 2 * modes)


def solution(mesh):
    placed = (
        P(None, ("gy", "gz"), None),
        P(None, ("gy", "gz"), None),
        P(None, None, "gy"),
        P("gy", None, "gz"),
        P(None, None, "gy", "gz"),
    )
    return jax.shard_map(
        per_device, mesh=mesh, in_specs=placed, out_specs=P(None, "gy", "gz"), check_vma=False
    )
```

profile of v0, /device:TPU:1, one launch (start us, length us, event | category | flops | bytes accessed | tf_op | source)
XLA Modules:
  0.0 185.7 jit_solution(2349157907954432843)
XLA Ops:
  0.0 1.1 stack.9
  3.1 7.6 %all-to-all-start = ((f32[8,2,1,3,512]{4,1,3,2,0:T(2,128)}), f32[8,2,1,3,512]{4,1,3,2,0:T(2,128)S(1)}, u32[]{:S(2)}, u32[]{:S(2)}) async-start(f32[8,2,1,3,512]{4,1,3,2,0:T(2,128)} %copy.237), calls=%async_computation | async-start | bytes 196608 | tf_op jit(solution)/shard_map/all_to_all | solution.py:30
  11.6 6.7 %all-to-all-done = f32[8,2,1,3,512]{4,1,3,2,0:T(2,128)S(1)} async-done(((f32[8,2,1,3,512]{4,1,3,2,0:T(2,128)}), f32[8,2,1,3,512]{4,1,3,2,0:T(2,128)S(1)}, u32[]{:S(2)}, u32[]{:S(2)}) %all-to-all-start) | async-done | bytes 98336 | tf_op jit(solution)/shard_map/all_to_all | solution.py:30
  18.3 3.4 %all-to-all-start.1 = ((f32[8,2,2,3,512]{4,1,3,2,0:T(2,128)}), f32[8,2,2,3,512]{4,1,3,2,0:T(2,128)S(1)}, u32[]{:S(2)}, u32[]{:S(2)}) async-start(f32[8,2,2,3,512]{4,1,3,2,0:T(2,128)} %copy.238), calls=%async_computation.1 | async-start | bytes 393216 | tf_op jit(solution)/shard_map/all_to_all | solution.py:30
  21.7 8.5 %all-to-all-done.1 = f32[8,2,2,3,512]{4,1,3,2,0:T(2,128)S(1)} async-done(((f32[8,2,2,3,512]{4,1,3,2,0:T(2,128)}), f32[8,2,2,3,512]{4,1,3,2,0:T(2,128)S(1)}, u32[]{:S(2)}, u32[]{:S(2)}) %all-to-all-start.1) | async-done | bytes 196640 | tf_op jit(solution)/shard_map/all_to_all | solution.py:30
  30.4 6.3 %collective-permute-start = (f32[2,3,2,512]{3,0,2,1:T(2,128)S(1)}, f32[2,3,2,512]{3,0,2,1:T(2,128)S(1)}, u32[]{:S(2)}, u32[]{:S(2)}) collective-permute-start(f32[2,3,2,512]{3,0,2,1:T(2,128)S(1)} %get-tuple-element.21), channel_id=1, source_target_pairs={{0,8},{8,16},{16,24},{24,32},{32,40},{40,48},{48,56},{56,64},{64,7... | collective-permute-start | bytes 73736 | tf_op jit(solution)/shard_map/ppermute | solution.py:42
  36.7 1.9 %collective-permute-start.1 = (f32[2,3,2,512]{3,0,2,1:T(2,128)S(1)}, f32[2,3,2,512]{3,0,2,1:T(2,128)S(1)}, u32[]{:S(2)}, u32[]{:S(2)}) collective-permute-start(f32[2,3,2,512]{3,0,2,1:T(2,128)S(1)} %get-tuple-element.22), channel_id=1, source_target_pairs={{8,0},{16,8},{24,16},{32,24},{40,32},{48,40},{56,48},{64,56},{72,6... | collective-permute-start | bytes 73736 | tf_op jit(solution)/shard_map/ppermute | solution.py:44
  38.7 2.2 %copy.331 = f32[24,24,256,1]{1,0,3,2:T(8,128)} copy(f32[24,24,256,1]{2,1,0,3:T(8,128)S(1)} %bitcast.275) | data formatting | bytes 1179648 | tf_op args[3]
  42.9 7.2 %convolution_bitcast_fusion = f32[3,24,256,2]{1,0,3,2:T(4,128)S(1)} fusion(f32[24,24,256,1]{1,0,3,2:T(8,128)} %copy.331, f32[3,24,256,2]{1,3,2,0:T(2,128)S(1)} %bitcast.254), kind=kOutput, calls=%fused_computation | convolution fusion | flops 10616832 | bytes 884736 | tf_op jit(solution)/shard_map/rcm,fcmp->frmp/dot_general | solution.py:160
  51.1 1.5 broadcast_in_dim.50
  52.6 15.5 %all-to-all-start.2 = ((f32[64,2048,2]{1,2,0:T(2,128)}), f32[64,2048,2]{1,2,0:T(2,128)S(1)}, u32[]{:S(2)}, u32[]{:S(2)}) async-start(f32[64,2048,2]{1,2,0:T(2,128)} %broadcast_in_dim.50), calls=%async_computation.2 | async-start | bytes 2097152 | tf_op jit(solution)/shard_map/all_to_all | solution.py:53
  69.2 27.0 %all-to-all-done.2 = f32[64,2048,2]{1,2,0:T(2,128)S(1)} async-done(((f32[64,2048,2]{1,2,0:T(2,128)}), f32[64,2048,2]{1,2,0:T(2,128)S(1)}, u32[]{:S(2)}, u32[]{:S(2)}) %all-to-all-start.2) | async-done | bytes 1048608 | tf_op jit(solution)/shard_map/all_to_all | solution.py:53
  96.6 5.3 %slice.563 = f32[32,2,2,256]{0,3,2,1:T(8,128)} slice(f32[64,2,2,256]{0,3,2,1:T(8,128)S(1)} %broadcast_select_fusion.1), slice={[1:64:2], [0:2:1], [0:2:1], [0:256:1]} | slice | bytes 262144 | tf_op jit(solution)/shard_map/slice | solution.py:76
  102.0 4.6 %slice.565 = f32[32,2,2,256]{0,3,2,1:T(8,128)S(1)} slice(f32[64,2,2,256]{0,3,2,1:T(8,128)S(1)} %broadcast_select_fusion.1), slice={[0:64:2], [0:2:1], [0:2:1], [0:256:1]} | slice | bytes 262144 | tf_op jit(solution)/shard_map/slice | solution.py:76
  112.9 2.2 %add_subtract_fusion.1 = f32[3,24,256,2]{1,0,3,2:T(4,128)S(1)} fusion(f32[3,24,256,2]{1,0,3,2:T(4,128)S(1)} %convolution_bitcast_fusion, f32[3,256,2]{0,2,1:T(2,128)S(1)} %bitcast.259, f32[24,256]{0,1:T(8,128)S(1)} %copy.284, f32[3,256,2]{0,2,1:T(2,128)S(1)} %bitcast.257, f32[24,256]{0,1:T(8,128)S(1)} %copy.244), kind=kLoop, calls=%fused_computation.3 | loop fusion | flops 147456 | bytes 356352 | tf_op jit(solution)/shard_map/sub | solution.py:169
  115.6 1.5 broadcast_in_dim.55
  117.0 6.3 %all-to-all-start.3 = ((f32[64,2048,2]{1,2,0:T(2,128)}), f32[64,2048,2]{1,2,0:T(2,128)S(1)}, u32[]{:S(2)}, u32[]{:S(2)}) async-start(f32[64,2048,2]{1,2,0:T(2,128)} %broadcast_in_dim.55), calls=%async_computation.3 | async-start | bytes 2097152 | tf_op jit(solution)/shard_map/all_to_all | solution.py:53
  124.8 26.6 %all-to-all-done.3 = f32[64,2048,2]{1,2,0:T(2,128)S(1)} async-done(((f32[64,2048,2]{1,2,0:T(2,128)}), f32[64,2048,2]{1,2,0:T(2,128)S(1)}, u32[]{:S(2)}, u32[]{:S(2)}) %all-to-all-start.3) | async-done | bytes 1048608 | tf_op jit(solution)/shard_map/all_to_all | solution.py:53
  152.6 1.1 broadcast_select_fusion
  153.7 5.2 %slice.627 = f32[32,2,2,256]{0,3,2,1:T(8,128)} slice(f32[64,2,2,256]{0,3,2,1:T(8,128)S(1)} %broadcast_select_fusion), slice={[0:63:2], [0:2:1], [0:2:1], [0:256:1]} | slice | bytes 262144 | tf_op jit(solution)/shard_map/slice | solution.py:76
  158.9 5.3 %slice.630 = f32[32,2,2,256]{0,3,2,1:T(8,128)} slice(f32[64,2,2,256]{0,3,2,1:T(8,128)S(1)} %broadcast_select_fusion), slice={[1:64:2], [0:2:1], [0:2:1], [0:256:1]} | slice | bytes 262144 | tf_op jit(solution)/shard_map/slice | solution.py:76
  166.4 1.8 fusion.15
  168.2 1.9 %slice.632 = f32[32,1,2,256]{0,3,2,1:T(8,128)S(1)} reverse(f32[32,1,2,256]{0,3,2,1:T(8,128)} %get-tuple-element.7), dimensions={0} | reverse | bytes 131072 | tf_op jit(solution)/shard_map/vmap()/slice | solution.py:140
  181.3 3.4 %add_subtract_fusion = f32[3,24,256,2]{1,0,3,2:T(4,128)S(1)} fusion(f32[3,256,2]{0,2,1:T(2,128)S(1)} %bitcast.266, f32[24,256]{0,1:T(8,128)} %copy.327, f32[3,256,2]{0,2,1:T(2,128)S(1)} %bitcast.265, f32[24,256]{0,1:T(8,128)S(1)} %copy-done.6, f32[3,24,256,2]{1,0,3,2:T(4,128)S(1)} %convolution_bitcast_fusion, f32[3,256,2]{0,2,1:T(2,128)S(1)} %bitcast.260, ...), kind=kLoop, calls=%fused_computation.2 | loop fusion | flops 294912 | bytes 417792 | tf_op jit(solution)/shard_map/sub | solution.py:172
  (256 shorter events, 29.9 us)
Async XLA Ops:
  0.0 21.7 %copy-start.7 = (f32[2,2,24,256]{3,2,1,0:T(8,128)S(1)}, f32[2,2,24,256]{3,2,1,0:T(8,128)}, u32[]{:S(2)}) copy-start(f32[2,2,24,256]{3,2,1,0:T(8,128)} %param.9) | copy-start | bytes 294916
  0.0 38.6 %copy-start.23 = (f32[2,5,24]{2,0,1:T(2,128)S(1)}, f32[2,5,24]{2,0,1:T(2,128)}, u32[]{:S(2)}) copy-start(f32[2,5,24]{2,0,1:T(2,128)} %param.7) | copy-start | bytes 2884
  0.0 38.6 %copy-start.2 = (f32[24,24,256]{2,1,0:T(8,128)S(1)}, f32[24,24,256]{2,1,0:T(8,128)}, u32[]{:S(2)}) copy-start(f32[24,24,256]{2,1,0:T(8,128)} %param.8) | copy-start | bytes 1769476
  3.1 15.2 %all-to-all-start = ((f32[8,2,1,3,512]{4,1,3,2,0:T(2,128)}), f32[8,2,1,3,512]{4,1,3,2,0:T(2,128)S(1)}, u32[]{:S(2)}, u32[]{:S(2)}) async-start(f32[8,2,1,3,512]{4,1,3,2,0:T(2,128)} %copy.237), calls=%async_computation | async-start | bytes 196608 | tf_op jit(solution)/shard_map/all_to_all | solution.py:30
  18.3 11.9 %all-to-all-start.1 = ((f32[8,2,2,3,512]{4,1,3,2,0:T(2,128)}), f32[8,2,2,3,512]{4,1,3,2,0:T(2,128)S(1)}, u32[]{:S(2)}, u32[]{:S(2)}) async-start(f32[8,2,2,3,512]{4,1,3,2,0:T(2,128)} %copy.238), calls=%async_computation.1 | async-start | bytes 393216 | tf_op jit(solution)/shard_map/all_to_all | solution.py:30
  30.4 10.7 %collective-permute-start = (f32[2,3,2,512]{3,0,2,1:T(2,128)S(1)}, f32[2,3,2,512]{3,0,2,1:T(2,128)S(1)}, u32[]{:S(2)}, u32[]{:S(2)}) collective-permute-start(f32[2,3,2,512]{3,0,2,1:T(2,128)S(1)} %get-tuple-element.21), channel_id=1, source_target_pairs={{0,8},{8,16},{16,24},{24,32},{32,40},{40,48},{48,56},{56,64},{64,7... | collective-permute-start | bytes 73736 | tf_op jit(solution)/shard_map/ppermute | solution.py:42
  36.7 5.1 %collective-permute-start.1 = (f32[2,3,2,512]{3,0,2,1:T(2,128)S(1)}, f32[2,3,2,512]{3,0,2,1:T(2,128)S(1)}, u32[]{:S(2)}, u32[]{:S(2)}) collective-permute-start(f32[2,3,2,512]{3,0,2,1:T(2,128)S(1)} %get-tuple-element.22), channel_id=1, source_target_pairs={{8,0},{16,8},{24,16},{32,24},{40,32},{48,40},{56,48},{64,56},{72,6... | collective-permute-start | bytes 73736 | tf_op jit(solution)/shard_map/ppermute | solution.py:44
  52.6 43.6 %all-to-all-start.2 = ((f32[64,2048,2]{1,2,0:T(2,128)}), f32[64,2048,2]{1,2,0:T(2,128)S(1)}, u32[]{:S(2)}, u32[]{:S(2)}) async-start(f32[64,2048,2]{1,2,0:T(2,128)} %broadcast_in_dim.50), calls=%async_computation.2 | async-start | bytes 2097152 | tf_op jit(solution)/shard_map/all_to_all | solution.py:53
  68.9 44.0 %copy-start = (f32[24,256]{0,1:T(8,128)}, f32[24,256]{0,1:T(8,128)S(1)}, u32[]{:S(2)}) copy-start(f32[24,256]{0,1:T(8,128)S(1)} %copy.284) | copy-start | bytes 73732
  112.9 10.5 %copy-start.12 = (f32[24,256]{1,0:T(8,128)S(1)}, f32[24,256]{1,0:T(8,128)}, u32[]{:S(2)}) copy-start(f32[24,256]{1,0:T(8,128)} %get-tuple-element.31) | copy-start | bytes 73732
  112.9 11.2 %copy-start.11 = (f32[24,256]{1,0:T(8,128)S(1)}, f32[24,256]{1,0:T(8,128)}, u32[]{:S(2)}) copy-start(f32[24,256]{1,0:T(8,128)} %get-tuple-element.34) | copy-start | bytes 73732
  117.0 34.4 %all-to-all-start.3 = ((f32[64,2048,2]{1,2,0:T(2,128)}), f32[64,2048,2]{1,2,0:T(2,128)S(1)}, u32[]{:S(2)}, u32[]{:S(2)}) async-start(f32[64,2048,2]{1,2,0:T(2,128)} %broadcast_in_dim.55), calls=%async_computation.3 | async-start | bytes 2097152 | tf_op jit(solution)/shard_map/all_to_all | solution.py:53
  124.8 41.6 %copy-start.24 = (pred[64]{0:T(512)(128)(4,1)}, pred[64]{0:T(512)(128)(4,1)S(1)}, u32[]{:S(2)}) copy-start(pred[64]{0:T(512)(128)(4,1)S(1)} %iota_compare_fusion) | copy-start | bytes 196
  171.3 2.0 %copy-start.4 = (f32[32,2,256]{2,1,0:T(2,128)}, f32[32,2,256]{2,1,0:T(2,128)S(1)}, u32[]{:S(2)}) copy-start(f32[32,2,256]{2,1,0:T(2,128)S(1)} %copy.294) | copy-start | bytes 196612
  175.5 2.3 %copy-start.3 = (f32[32,2,256]{2,1,0:T(2,128)S(1)}, f32[32,2,256]{2,1,0:T(2,128)}, u32[]{:S(2)}) copy-start(f32[32,2,256]{2,1,0:T(2,128)} %copy.292) | copy-start | bytes 196612
  175.5 2.3 %copy-start.5 = (f32[32,2,256]{2,1,0:T(2,128)S(1)}, f32[32,2,256]{2,1,0:T(2,128)}, u32[]{:S(2)}) copy-start(f32[32,2,256]{2,1,0:T(2,128)} %copy-done.4) | copy-start | bytes 196612
  177.5 3.1 %copy-start.14 = (f32[4,2,256]{2,1,0:T(2,128)S(1)}, f32[4,2,256]{2,1,0:T(2,128)}, u32[]{:S(2)}) copy-start(f32[4,2,256]{2,1,0:T(2,128)} %copy-done.13) | copy-start | bytes 24580
  177.5 3.1 %copy-start.16 = (f32[4,2,256]{2,1,0:T(2,128)S(1)}, f32[4,2,256]{2,1,0:T(2,128)}, u32[]{:S(2)}) copy-start(f32[4,2,256]{2,1,0:T(2,128)} %copy-done.15) | copy-start | bytes 24580
  177.6 3.2 %copy-start.18 = (f32[2,2,256]{2,1,0:T(2,128)S(1)}, f32[2,2,256]{2,1,0:T(2,128)}, u32[]{:S(2)}) copy-start(f32[2,2,256]{2,1,0:T(2,128)} %copy-done.17) | copy-start | bytes 12292
  177.6 3.2 %copy-start.20 = (f32[2,2,256]{2,1,0:T(2,128)S(1)}, f32[2,2,256]{2,1,0:T(2,128)}, u32[]{:S(2)}) copy-start(f32[2,2,256]{2,1,0:T(2,128)} %copy-done.19) | copy-start | bytes 12292
  177.6 3.3 %copy-start.21 = (f32[2,256]{1,0:T(2,128)S(1)}, f32[2,256]{1,0:T(2,128)}, u32[]{:S(2)}) copy-start(f32[2,256]{1,0:T(2,128)} %get-tuple-element.93) | copy-start | bytes 6148
  177.6 3.3 %copy-start.22 = (f32[2,256]{1,0:T(2,128)S(1)}, f32[2,256]{1,0:T(2,128)}, u32[]{:S(2)}) copy-start(f32[2,256]{1,0:T(2,128)} %get-tuple-element.94) | copy-start | bytes 6148
  177.8 3.5 %copy-start.1 = (f32[24,256]{0,1:T(8,128)S(1)}, f32[24,256]{0,1:T(8,128)}, u32[]{:S(2)}) copy-start(f32[24,256]{0,1:T(8,128)} %copy-done) | copy-start | bytes 73732
  177.8 3.5 %copy-start.6 = (f32[24,256]{0,1:T(8,128)S(1)}, f32[24,256]{0,1:T(8,128)}, u32[]{:S(2)}) copy-start(f32[24,256]{0,1:T(8,128)} %copy.287) | copy-start | bytes 73732
  (7 other events, 4.2 us)
where the time goes:
time: 187 us; the launch traced here: 186 us
  waiting for transfers between devices  69.5 us (37%)
  local copies, waits for them, and re-layouts  52.1 us (28%)
  starting transfers between devices  41 us (22%)
  other arithmetic  14.2 us (8%)
  matrix products  7.18 us (4%)
    all_to_all x2, waiting for transfers between devices, copy_for_each(): return lax.all_to_all(copies, axis, split_axis=0, concat_axis=0, tiled=True)  53.6 us
    all_to_all x2, starting transfers between devices, copy_for_each(): return lax.all_to_all(copies, axis, split_axis=0, concat_axis=0, tiled=True)  21.7 us
    slice x22, local copies, waits for them, and re-layouts, joined_by_halves(): part[side::2]  21 us
    all_to_all x2, waiting for transfers between devices, several_exchanges(): lax.all_to_all(section, axis, split_axis=0, concat_axis=0, tiled=True)  15.2 us
    all_to_all x2, starting transfers between devices, several_exchanges(): lax.all_to_all(section, axis, split_axis=0, concat_axis=0, tiled=True)  11 us
    dot_general x1, matrix products, per_device(): jnp.einsum('rcm,fcmp->frmp', inverse, rhs_modes, precision=lax.Precision....  7.18 us
    ppermute x1, starting transfers between devices, extended(): lax.ppermute(tail, axis, [(i, (i + 1) % count) for i in range(ends)])  6.27 us
    slice x10, local copies, waits for them, and re-layouts, compose(): earlier[..., 0, :, :][..., None, :, :]  3.89 us
  transfers between devices with their start and end apart: 6, of which 5 were waited for; matrix products, arithmetic and copies ran while one was open for 3% of the time, Pallas kernels for 0%

commit v1 on v0

v1 whole, which is shorter than its diff:
```python
import functools

import jax
import jax.numpy as jnp
from jax import lax
from jax.experimental import pallas as pl
from jax.experimental.pallas import tpu as pltpu
from jax.sharding import PartitionSpec as P

MESH = pl.DeviceIdType.MESH
F32 = jnp.float32


def kernel(
    vel, exp, bands, inv, spk, out,
    rv, re, hv, he, inv_h, inv_t, spk_h, spk_d, coef, vx, ex, rhs, local,
    map_s, map_r, gmap_s, gmap_r, cd_s, cd_r, gcd_s, gcd_r, ts_s, ts_r,
    base_t, base_s, base_r, zero_t, zero_s, t_in, s_in,
    ld_sem, own_sem, rv_send, rv_recv, re_send, re_recv, h_send, h_recv,
    m_send, m_recv, gm_send, gm_recv, c_send, c_recv, gc_send, gc_recv, ts_send, ts_recv,
):
    gy = lax.axis_index("gy")
    gz = lax.axis_index("gz")
    zi = gy // 8
    pi = gy % 8
    xj = pi // 2
    co = pi % 2

    def to_y(k):
        return {"gz": (gz + k) % 8}

    def to_plane(k):
        return {"gy": zi * 8 + (pi + k) % 8}

    def to_z(k):
        return {"gy": ((zi + k) % 8) * 8 + pi}

    def to_next(k):
        return {"gy": (gy + k + 64) % 64}

    def remote(src, dst, send, recv, where):
        return pltpu.make_async_remote_copy(
            src_ref=src, dst_ref=dst, send_sem=send, recv_sem=recv,
            device_id=where, device_id_type=MESH,
        )

    loads = []
    for h in range(2):
        loads.append(pltpu.make_async_copy(spk.at[:, pl.ds(h * 128, 128)], spk_h.at[h], ld_sem.at[h]))
    for h in range(2):
        loads.append(pltpu.make_async_copy(inv.at[:, pl.ds(h * 128, 128)], inv_h.at[h], ld_sem.at[2 + h]))
    for copy in loads:
        copy.start()
    mine = pl.ds(pl.multiple_of(gz * 512, 512), 512)
    own_v = pltpu.make_async_copy(vel.at[:, :, mine], rv.at[gz], rv_recv.at[0])
    own_e = pltpu.make_async_copy(exp.at[:, :, mine], re.at[gz], re_recv.at[0])
    own_v.start()
    own_e.start()

    barrier = pltpu.get_barrier_semaphore()
    for k in range(1, 8):
        for where in (to_y(k), to_z(k), to_plane(k)):
            pl.semaphore_signal(barrier, inc=1, device_id=where, device_id_type=MESH)
    for k in (-1, 1):
        pl.semaphore_signal(barrier, inc=1, device_id=to_next(k), device_id_type=MESH)
    pl.semaphore_wait(barrier, 23)

    sends = []
    for k in (4, 3, 5, 2, 6, 1, 7):
        cols = pl.ds(pl.multiple_of(((gz + k) % 8) * 512, 512), 512)
        for src, dst, send, recv in ((vel, rv, rv_send, rv_recv), (exp, re, re_send, re_recv)):
            copy = remote(src.at[:, :, cols], dst.at[gz], send.at[k], recv.at[k], to_y(k))
            copy.start()
            sends.append(copy)

    lane = lax.broadcasted_iota(jnp.int32, (24, 128), 1) // 2
    for h in range(2):
        loads[h].wait()

    def double_spikes(i, carry):
        row = pl.multiple_of(i * 24, 8)
        for h in range(2):
            part = spk_h[h, pl.ds(row, 24), :]
            for j in range(2):
                spk_d[2 * h + j, pl.ds(row, 24), :] = jnp.take_along_axis(part, lane + 64 * j, axis=1)
        return carry

    lax.fori_loop(0, 4, double_spikes, 0)
    for lt in range(4):
        for k in range(2):
            for q in range(2):
                i = 2 * k + q
                map_s[lt, i : i + 1, :] = -spk_d[lt, q * 24 + 22 + k : q * 24 + 23 + k, :]
                map_s[lt, 4 + i : 5 + i, :] = -spk_d[lt, q * 24 + k : q * 24 + k + 1, :]
                map_s[lt, 8 + i : 9 + i, :] = -spk_d[lt, 48 + q * 24 + k : 48 + q * 24 + k + 1, :]
    map_r[pi] = map_s[xj]
    for k in range(1, 8):
        copy = remote(
            map_s.at[(pi + k) % 8 // 2], map_r.at[pi], m_send.at[k], m_recv.at[k], to_plane(k)
        )
        copy.start()
        sends.append(copy)

    eye = lax.broadcasted_iota(jnp.int32, (24, 24), 0) == lax.broadcasted_iota(jnp.int32, (24, 24), 1)
    for d in range(5):
        first = bands[d : d + 1, :]
        second = bands[5 + d : 6 + d, :]
        for i, row in ((d, first + second), (5 + d, first)):
            column = jnp.sum(jnp.where(eye, row, 0.0), axis=1, keepdims=True)
            coef[i] = jnp.broadcast_to(column, (24, 128))

    for h in range(2):
        loads[2 + h].wait()

    def turn(c, carry):
        for h in range(2):
            part = inv_h[h, pl.ds(c, 24, stride=24), :]
            for j in range(2):
                inv_t[2 * h + j, c] = jnp.take_along_axis(part, lane + 64 * j, axis=1)
        return carry

    lax.fori_loop(0, 24, turn, 0)

    def apply2(maps, at, first, second):
        return (
            maps[at : at + 1, :] * first + maps[at + 1 : at + 2, :] * second,
            maps[at + 2 : at + 3, :] * first + maps[at + 3 : at + 4, :] * second,
        )

    for k in range(1, 8):
        remote(map_s.at[0], map_r.at[(pi - k + 8) % 8], m_send.at[k], m_recv.at[k], to_plane(k)).wait_recv()
    col = lax.broadcasted_iota(jnp.int32, (2, 128), 0)
    unit = (jnp.where(col == 0, 1.0, 0.0), jnp.where(col == 1, 1.0, 0.0))
    t0, t1 = unit
    for b in range(8):
        base_t[b, 0:2] = t0
        base_t[b, 2:4] = t1
        t0, t1 = apply2(map_r[b], 0, t0, t1)
    s0 = s1 = jnp.zeros((2, 128), F32)
    r0, r1 = unit
    gmap_s[0:2] = t0
    gmap_s[2:4] = t1
    for b in range(7, -1, -1):
        maps = map_r[b]
        base_s[b, 0:2] = s0
        base_s[b, 2:4] = s1
        base_r[b, 0:2] = r0
        base_r[b, 2:4] = r1
        w0, w1 = apply2(maps, 4, base_t[b, 0:2], base_t[b, 2:4])
        u0, u1 = apply2(maps, 8, s0, s1)
        s0, s1 = w0 + u0, w1 + u1
        r0, r1 = apply2(maps, 8, r0, r1)
    gmap_s[4:6] = s0
    gmap_s[6:8] = s1
    gmap_s[8:10] = r0
    gmap_s[10:12] = r1
    gmap_r[zi] = gmap_s[...]
    for k in range(1, 8):
        copy = remote(gmap_s, gmap_r.at[zi], gm_send.at[k], gm_recv.at[k], to_z(k))
        copy.start()
        sends.append(copy)

    own_v.wait()
    own_e.wait()
    for k in range(1, 8):
        slot = (gz - k + 8) % 8
        cols = pl.ds(0, 512)
        remote(vel.at[:, :, cols], rv.at[slot], rv_send.at[k], rv_recv.at[k], to_y(k)).wait_recv()
        remote(exp.at[:, :, cols], re.at[slot], re_send.at[k], re_recv.at[k], to_y(k)).wait_recv()
    halos = []
    for side, slot, step in ((0, 7, 1), (1, 0, -1)):
        for a, (src, dst) in enumerate(((rv, hv), (re, he))):
            i = 2 * side + a
            copy = remote(src.at[slot], dst.at[side], h_send.at[i], h_recv.at[i], to_next(step))
            copy.start()
            sends.append(copy)
            halos.append(copy)

    def gather_rows(lt, carry):
        cols = pl.ds(pl.multiple_of(lt * 128, 128), 128)
        for got, rows in ((rv, vx), (re, ex)):
            for g in range(8):
                for f in range(3):
                    rows[lt, f, 2 + 3 * g : 5 + 3 * g, :] = got[g, f, :, cols]
        return carry

    lax.fori_loop(0, 4, gather_rows, 0)
    for copy in halos:
        copy.wait_recv()

    def gather_edges(lt, carry):
        cols = pl.ds(pl.multiple_of(lt * 128, 128), 128)
        for got, rows in ((hv, vx), (he, ex)):
            for f in range(3):
                rows[lt, f, 0:2, :] = jnp.where(gy > 0, got[0, f, 1:3, cols], 0.0)
                rows[lt, f, 26:28, :] = jnp.where(gy < 63, got[1, f, 0:2, cols], 0.0)
        return carry

    lax.fori_loop(0, 4, gather_edges, 0)

    def solve(lt, carry):
        for f in range(3):
            total = jnp.zeros((24, 128), F32)
            for d in range(5):
                total = total + coef[d] * vx[lt, f, d : d + 24, :]
                total = total + coef[5 + d] * ex[lt, f, d : d + 24, :]
            rhs[lt, f] = total
        sums = [jnp.zeros((24, 128), F32) for _ in range(3)]
        for c in range(24):
            weight = inv_t[lt, c]
            for f in range(3):
                sums[f] = sums[f] + weight * rhs[lt, f, c : c + 1, :]
        for f in range(3):
            local[lt, f] = sums[f]
            for k in range(2):
                cd_s[lt, 3 * k + f : 3 * k + f + 1, :] = sums[f][22 + k : 23 + k, :]
                cd_s[lt, 6 + 3 * k + f : 7 + 3 * k + f, :] = sums[f][k : k + 1, :]
        return carry

    lax.fori_loop(0, 4, solve, 0)

    for k in range(1, 8):
        copy = remote(
            cd_s.at[(pi + k) % 8 // 2], cd_r.at[pi], c_send.at[k], c_recv.at[k], to_plane(k)
        )
        copy.start()
        sends.append(copy)
    cd_r[pi] = cd_s[xj]
    for k in range(1, 8):
        remote(gmap_s, gmap_r.at[(zi - k + 8) % 8], gm_send.at[k], gm_recv.at[k], to_z(k)).wait_recv()
    for k in range(1, 8):
        remote(cd_s.at[0], cd_r.at[(pi - k + 8) % 8], c_send.at[k], c_recv.at[k], to_plane(k)).wait_recv()
    t0 = t1 = jnp.zeros((3, 128), F32)
    for b in range(8):
        zero_t[b, 0:3] = t0
        zero_t[b, 3:6] = t1
        n0, n1 = apply2(map_r[b], 0, t0, t1)
        t0, t1 = n0 + cd_r[b, 0:3, :], n1 + cd_r[b, 3:6, :]
    gcd_s[0:3] = t0
    gcd_s[3:6] = t1
    s0 = s1 = jnp.zeros((3, 128), F32)
    for b in range(7, -1, -1):
        zero_s[b, 0:3] = s0
        zero_s[b, 3:6] = s1
        w0, w1 = apply2(map_r[b], 4, zero_t[b, 0:3], zero_t[b, 3:6])
        u0, u1 = apply2(map_r[b], 8, s0, s1)
        s0, s1 = u0 + (w0 + cd_r[b, 6:9, :]), u1 + (w1 + cd_r[b, 9:12, :])
    gcd_s[6:9] = s0
    gcd_s[9:12] = s1

    for k in range(1, 8):
        copy = remote(gcd_s, gcd_r.at[zi], gc_send.at[k], gc_recv.at[k], to_z(k))
        copy.start()
        sends.append(copy)
    gcd_r[zi] = gcd_s[...]
    for k in range(1, 8):
        remote(gcd_s, gcd_r.at[(zi - k + 8) % 8], gc_send.at[k], gc_recv.at[k], to_z(k)).wait_recv()
    t0 = t1 = jnp.zeros((3, 128), F32)
    for g in range(8):
        t_in[g, 0:3] = t0
        t_in[g, 3:6] = t1
        n0, n1 = apply2(gmap_r[g], 0, t0, t1)
        t0, t1 = n0 + gcd_r[g, 0:3, :], n1 + gcd_r[g, 3:6, :]
    s0 = s1 = jnp.zeros((3, 128), F32)
    for g in range(7, -1, -1):
        s_in[g, 0:3] = s0
        s_in[g, 3:6] = s1
        w0, w1 = apply2(gmap_r[g], 4, t_in[g, 0:3], t_in[g, 3:6])
        u0, u1 = apply2(gmap_r[g], 8, s0, s1)
        s0, s1 = u0 + (w0 + gcd_r[g, 6:9, :]), u1 + (w1 + gcd_r[g, 9:12, :])

    t0, t1 = t_in[zi, 0:3], t_in[zi, 3:6]
    s0, s1 = s_in[zi, 0:3], s_in[zi, 3:6]

    def mapped(base, b, first, second):
        return (
            base[b, 0:1] * first + base[b, 1:2] * second,
            base[b, 2:3] * first + base[b, 3:4] * second,
        )

    for b in range(8):
        a0, a1 = mapped(base_t, b, t0, t1)
        ts_s[b, 0:3] = zero_t[b, 0:3] + a0
        ts_s[b, 3:6] = zero_t[b, 3:6] + a1
        a0, a1 = mapped(base_s, b, t0, t1)
        b0, b1 = mapped(base_r, b, s0, s1)
        ts_s[b, 6:9] = zero_s[b, 0:3] + a0 + b0
        ts_s[b, 9:12] = zero_s[b, 3:6] + a1 + b1
    backs = []
    for k in range(1, 4):
        copy = remote(
            ts_s.at[(pi + 2 * k) % 8], ts_r.at[xj], ts_send.at[k], ts_recv.at[k], to_plane(2 * k)
        )
        copy.start()
        sends.append(copy)
    ts_r[xj] = ts_s[pi]
    for k in range(1, 4):
        remote(
            ts_s.at[0], ts_r.at[(xj - k + 4) % 4], ts_send.at[k], ts_recv.at[k], to_plane(2 * k)
        ).wait_recv()

    for lt in range(4):
        for f in range(3):
            value = local[lt, f]
            for k in range(2):
                value = value - spk_d[lt, k * 24 : k * 24 + 24, :] * ts_r[lt, 3 * k + f : 3 * k + f + 1, :]
            for k in range(2):
                value = value - spk_d[lt, 48 + k * 24 : 72 + k * 24, :] * ts_r[lt, 6 + 3 * k + f : 7 + 3 * k + f, :]
            out[f, :, lt * 128 : lt * 128 + 128] = value
    for copy in sends:
        copy.wait_send()


def per_device(velocity, explicit, bands, inverse, spikes):
    dma = pltpu.SemaphoreType.DMA
    vmem = lambda *shape: pltpu.VMEM(shape, F32)
    hbm = pl.BlockSpec(memory_space=pl.ANY)
    return pl.pallas_call(
        kernel,
        out_shape=jax.ShapeDtypeStruct((3, 24, 512), F32),
        in_specs=[hbm, hbm, pl.BlockSpec(memory_space=pltpu.VMEM), hbm, hbm],
        out_specs=pl.BlockSpec(memory_space=pltpu.VMEM),
        scratch_shapes=[
            vmem(8, 3, 3, 512), vmem(8, 3, 3, 512), vmem(2, 3, 3, 512), vmem(2, 3, 3, 512),
            vmem(2, 576, 128), vmem(4, 24, 24, 128), vmem(2, 96, 128), vmem(4, 96, 128),
            vmem(10, 24, 128), vmem(4, 3, 32, 128), vmem(4, 3, 32, 128),
            vmem(4, 3, 24, 128), vmem(4, 3, 24, 128),
            vmem(4, 12, 128), vmem(8, 12, 128), vmem(12, 128), vmem(8, 12, 128),
            vmem(4, 12, 128), vmem(8, 12, 128), vmem(12, 128), vmem(8, 12, 128),
            vmem(8, 12, 128), vmem(4, 12, 128),
            vmem(8, 4, 128), vmem(8, 4, 128), vmem(8, 4, 128),
            vmem(8, 6, 128), vmem(8, 6, 128), vmem(8, 6, 128), vmem(8, 6, 128),
            dma((4,)), dma((2,)), dma((8,)), dma((8,)), dma((8,)), dma((8,)), dma((4,)), dma((4,)),
            dma((8,)), dma((8,)), dma((8,)), dma((8,)), dma((8,)), dma((8,)), dma((8,)), dma((8,)),
            dma((4,)), dma((4,)),
        ],
        compiler_params=pltpu.CompilerParams(collective_id=0, has_side_effects=True),
    )(velocity, explicit, bands.reshape(10, 24), inverse.reshape(576, 256), spikes.reshape(96, 256))


def solution(mesh):
    placed = (
        P(None, ("gy", "gz"), None),
        P(None, ("gy", "gz"), None),
        P(None, None, "gy"),
        P("gy", None, "gz"),
        P(None, None, "gy", "gz"),
    )
    return jax.shard_map(
        per_device, mesh=mesh, in_specs=placed, out_specs=P(None, "gy", "gz"), check_vma=False
    )
```

time: 187 us -> 46.2 us (0.25)
  the two profiles are of different devices: /device:TPU:1 before, /device:TPU:24 now
where the time goes in v1:
time: 46.2 us; the launch traced here: 45.9 us
  Pallas kernels  43.1 us (93%)
  local copies, waits for them, and re-layouts  2.87 us (6%)
    pallas_call x1, Pallas kernels, per_device(): pl.pallas_call(kernel, out_shape=jax.ShapeDtypeStruct((3, 24, 512), F32),...  43.1 us
    unnamed x2, local copies, waits for them, and re-layouts  2.27 us

profile of v1, /device:TPU:24, one launch (start us, length us, event | category | flops | bytes accessed | tf_op | source)
XLA Modules:
  0.0 45.9 jit_solution(7120556951832157506)
XLA Ops:
  0.0 0.7 %copy.7 = f32[2,5,24]{2,1,0:T(8,128)S(1)} copy(f32[2,5,24]{2,0,1:T(2,128)} %param.7) | data formatting | bytes 1920 | tf_op args[2]
  0.7 0.6 %reshape.9.bands = f32[10,24]{1,0:T(8,128)} reshape(f32[2,5,24]{2,1,0:T(8,128)S(1)} %copy.7) | data formatting | bytes 1920 | tf_op jit(solution)/shard_map/reshape | solution.py:338
  1.3 43.1 %shard_map.55 = f32[3,24,512]{2,1,0:T(8,128)} custom-call(f32[3,3,4096]{2,1,0:T(4,128)} %vel.1, f32[3,3,4096]{2,1,0:T(4,128)} %exp.1, f32[10,24]{1,0:T(8,128)} %reshape.9.bands, f32[576,256]{1,0:T(8,128)} %bitcast.2, f32[96,256]{1,0:T(8,128)} %bitcast.3), custom_call_target="tpu_custom_call" | custom-call | tf_op jit(solution)/shard_map/pallas_call | solution.py:318
  44.4 1.6 %copy.9 = f32[3,24,512]{2,1,0:T(8,128)} copy(f32[3,24,512]{2,1,0:T(8,128)} %shard_map.55) | data formatting | bytes 294912

commit v2 on v1

--- a/solution.py
+++ b/solution.py
@@ -12,8 +12,8 @@
 
 
 def kernel(
-    vel, exp, bands, inv, spk, out,
-    rv, re, hv, he, inv_h, inv_t, spk_h, spk_d, coef, vx, ex, rhs, local,
+    vel, exp, bands_in, inv, spk, out,
+    bands, rv, re, hv, he, inv_h, inv_t, spk_h, spk_d, coef, vx, ex, rhs, local,
     map_s, map_r, gmap_s, gmap_r, cd_s, cd_r, gcd_s, gcd_r, ts_s, ts_r,
     base_t, base_s, base_r, zero_t, zero_s, t_in, s_in,
     ld_sem, own_sem, rv_send, rv_recv, re_send, re_recv, h_send, h_recv,
@@ -49,6 +49,7 @@
         loads.append(pltpu.make_async_copy(spk.at[:, pl.ds(h * 128, 128)], spk_h.at[h], ld_sem.at[h]))
     for h in range(2):
         loads.append(pltpu.make_async_copy(inv.at[:, pl.ds(h * 128, 128)], inv_h.at[h], ld_sem.at[2 + h]))
+    loads.append(pltpu.make_async_copy(bands_in, bands, ld_sem.at[4]))
     for copy in loads:
         copy.start()
     mine = pl.ds(pl.multiple_of(gz * 512, 512), 512)
@@ -102,24 +103,13 @@
         sends.append(copy)
 
     eye = lax.broadcasted_iota(jnp.int32, (24, 24), 0) == lax.broadcasted_iota(jnp.int32, (24, 24), 1)
+    loads[4].wait()
     for d in range(5):
-        first = bands[d : d + 1, :]
-        second = bands[5 + d : 6 + d, :]
+        first = bands[d, 0:1, :]
+        second = bands[d, 1:2, :]
         for i, row in ((d, first + second), (5 + d, first)):
             column = jnp.sum(jnp.where(eye, row, 0.0), axis=1, keepdims=True)
             coef[i] = jnp.broadcast_to(column, (24, 128))
-
-    for h in range(2):
-        loads[2 + h].wait()
-
-    def turn(c, carry):
-        for h in range(2):
-            part = inv_h[h, pl.ds(c, 24, stride=24), :]
-            for j in range(2):
-                inv_t[2 * h + j, c] = jnp.take_along_axis(part, lane + 64 * j, axis=1)
-        return carry
-
-    lax.fori_loop(0, 24, turn, 0)
 
     def apply2(maps, at, first, second):
         return (
@@ -160,15 +150,14 @@
         copy.start()
         sends.append(copy)
 
-    own_v.wait()
-    own_e.wait()
-    for k in range(1, 8):
-        slot = (gz - k + 8) % 8
-        cols = pl.ds(0, 512)
-        remote(vel.at[:, :, cols], rv.at[slot], rv_send.at[k], rv_recv.at[k], to_y(k)).wait_recv()
-        remote(exp.at[:, :, cols], re.at[slot], re_send.at[k], re_recv.at[k], to_y(k)).wait_recv()
+    def wait_slot(slot):
+        k = (gz - slot + 8) % 8
+        pltpu.make_async_copy(rv.at[slot], rv.at[slot], rv_recv.at[k]).wait()
+        pltpu.make_async_copy(re.at[slot], re.at[slot], re_recv.at[k]).wait()
+
     halos = []
     for side, slot, step in ((0, 7, 1), (1, 0, -1)):
+        wait_slot(slot)
         for a, (src, dst) in enumerate(((rv, hv), (re, he))):
             i = 2 * side + a
             copy = remote(src.at[slot], dst.at[side], h_send.at[i], h_recv.at[i], to_next(step))
@@ -176,15 +165,33 @@
             sends.append(copy)
             halos.append(copy)
 
-    def gather_rows(lt, carry):
-        cols = pl.ds(pl.multiple_of(lt * 128, 128), 128)
-        for got, rows in ((rv, vx), (re, ex)):
-            for g in range(8):
+    for h in range(2):
+        loads[2 + h].wait()
+
+    def turn(c, carry):
+        for h in range(2):
+            part = inv_h[h, pl.ds(c, 24, stride=24), :]
+            for j in range(2):
+                inv_t[2 * h + j, c] = jnp.take_along_axis(part, lane + 64 * j, axis=1)
+        return carry
+
+    lax.fori_loop(0, 24, turn, 0)
+
+    def gather_rows(g):
+        def body(lt, carry):
+            cols = pl.ds(pl.multiple_of(lt * 128, 128), 128)
+            for got, rows in ((rv, vx), (re, ex)):
                 for f in range(3):
                     rows[lt, f, 2 + 3 * g : 5 + 3 * g, :] = got[g, f, :, cols]
-        return carry
-
-    lax.fori_loop(0, 4, gather_rows, 0)
+            return carry
+
+        lax.fori_loop(0, 4, body, 0)
+
+    gather_rows(7)
+    gather_rows(0)
+    for g in (3, 4, 2, 5, 1, 6):
+        wait_slot(g)
+        gather_rows(g)
     for copy in halos:
         copy.wait_recv()
 
@@ -278,22 +285,22 @@
             base[b, 2:3] * first + base[b, 3:4] * second,
         )
 
-    for b in range(8):
+    for j in range(4):
+        b = 2 * j + co
         a0, a1 = mapped(base_t, b, t0, t1)
-        ts_s[b, 0:3] = zero_t[b, 0:3] + a0
-        ts_s[b, 3:6] = zero_t[b, 3:6] + a1
+        ts_s[j, 0:3] = zero_t[b, 0:3] + a0
+        ts_s[j, 3:6] = zero_t[b, 3:6] + a1
         a0, a1 = mapped(base_s, b, t0, t1)
         b0, b1 = mapped(base_r, b, s0, s1)
-        ts_s[b, 6:9] = zero_s[b, 0:3] + a0 + b0
-        ts_s[b, 9:12] = zero_s[b, 3:6] + a1 + b1
-    backs = []
+        ts_s[j, 6:9] = zero_s[b, 0:3] + a0 + b0
+        ts_s[j, 9:12] = zero_s[b, 3:6] + a1 + b1
     for k in range(1, 4):
         copy = remote(
-            ts_s.at[(pi + 2 * k) % 8], ts_r.at[xj], ts_send.at[k], ts_recv.at[k], to_plane(2 * k)
-        )
-        copy.start()
-        sends.append(copy)
-    ts_r[xj] = ts_s[pi]
+            ts_s.at[(xj + k) % 4], ts_r.at[xj], ts_send.at[k], ts_recv.at[k], to_plane(2 * k)
+        )
+        copy.start()
+        sends.append(copy)
+    ts_r[xj] = ts_s[xj]
     for k in range(1, 4):
         remote(
             ts_s.at[0], ts_r.at[(xj - k + 4) % 4], ts_send.at[k], ts_recv.at[k], to_plane(2 * k)
@@ -314,13 +321,18 @@
 def per_device(velocity, explicit, bands, inverse, spikes):
     dma = pltpu.SemaphoreType.DMA
     vmem = lambda *shape: pltpu.VMEM(shape, F32)
-    hbm = pl.BlockSpec(memory_space=pl.ANY)
+    hbm = pl.BlockSpec(memory_space=pltpu.HBM)
+    operands = [
+        pltpu.with_memory_space_constraint(a, pltpu.HBM)
+        for a in (velocity, explicit, bands.transpose(1, 0, 2), inverse.reshape(576, 256), spikes.reshape(96, 256))
+    ]
     return pl.pallas_call(
         kernel,
         out_shape=jax.ShapeDtypeStruct((3, 24, 512), F32),
-        in_specs=[hbm, hbm, pl.BlockSpec(memory_space=pltpu.VMEM), hbm, hbm],
+        in_specs=[hbm] * 5,
         out_specs=pl.BlockSpec(memory_space=pltpu.VMEM),
         scratch_shapes=[
+            vmem(5, 2, 24),
             vmem(8, 3, 3, 512), vmem(8, 3, 3, 512), vmem(2, 3, 3, 512), vmem(2, 3, 3, 512),
             vmem(2, 576, 128), vmem(4, 24, 24, 128), vmem(2, 96, 128), vmem(4, 96, 128),
             vmem(10, 24, 128), vmem(4, 3, 32, 128), vmem(4, 3, 32, 128),
@@ -330,12 +342,12 @@
             vmem(8, 12, 128), vmem(4, 12, 128),
             vmem(8, 4, 128), vmem(8, 4, 128), vmem(8, 4, 128),
             vmem(8, 6, 128), vmem(8, 6, 128), vmem(8, 6, 128), vmem(8, 6, 128),
-            dma((4,)), dma((2,)), dma((8,)), dma((8,)), dma((8,)), dma((8,)), dma((4,)), dma((4,)),
+            dma((5,)), dma((2,)), dma((8,)), dma((8,)), dma((8,)), dma((8,)), dma((4,)), dma((4,)),
             dma((8,)), dma((8,)), dma((8,)), dma((8,)), dma((8,)), dma((8,)), dma((8,)), dma((8,)),
             dma((4,)), dma((4,)),
         ],
-        compiler_params=pltpu.CompilerParams(collective_id=0, has_side_effects=True),
-    )(velocity, explicit, bands.reshape(10, 24), inverse.reshape(576, 256), spikes.reshape(96, 256))
+        compiler_params=pltpu.CompilerParams(collective_id=0, has_side_effects=True, vmem_limit_bytes=16 * 1024 * 1024),
+    )(*operands)
 
 
 def solution(mesh):

time: 46.2 us -> 41 us (0.89)
  the two profiles are of different devices: /device:TPU:24 before, /device:TPU:1 now
where the time goes in v2:
time: 41 us; the launch traced here: 40.9 us
  Pallas kernels  40.3 us (98%)
  local copies, waits for them, and re-layouts  0.66 us (2%)
    pallas_call x1, Pallas kernels, per_device(): pl.pallas_call(kernel, out_shape=jax.ShapeDtypeStruct((3, 24, 512), F32),...  40.3 us

profile of v2, /device:TPU:1, one launch (start us, length us, event | category | flops | bytes accessed | tf_op | source)
XLA Modules:
  0.0 40.9 jit_solution(7677509369364631119)
XLA Ops:
  0.0 40.3 %shard_map.55 = f32[3,24,512]{2,1,0:T(8,128)S(1)} custom-call(f32[3,3,4096]{2,1,0:T(4,128)} %vel.1, f32[3,3,4096]{2,1,0:T(4,128)} %exp.1, f32[5,2,24]{2,1,0:T(2,128)} %bitcast.5, f32[576,256]{1,0:T(8,128)} %bitcast.3, f32[96,256]{1,0:T(8,128)} %bitcast.4), custom_call_target="tpu_custom_call" | custom-call | tf_op jit(solution)/shard_map/pallas_call | solution.py:329
  40.3 0.7 %copy.7 = f32[3,24,512]{2,1,0:T(8,128)} copy(f32[3,24,512]{2,1,0:T(8,128)S(1)} %shard_map.55) | data formatting | bytes 294912

commit v3 on v2

--- a/solution.py
+++ b/solution.py
@@ -13,9 +13,9 @@
 
 def kernel(
     vel, exp, bands_in, inv, spk, out,
-    bands, rv, re, hv, he, inv_h, inv_t, spk_h, spk_d, coef, vx, ex, rhs, local,
+    bands, vs, es, rv, re, hv, he, inv_h, inv_t, spk_h, spk_d, coef, vx, ex, rhs, local,
     map_s, map_r, gmap_s, gmap_r, cd_s, cd_r, gcd_s, gcd_r, ts_s, ts_r,
-    base_t, base_s, base_r, zero_t, zero_s, t_in, s_in,
+    base_t, base_s, base_r, zero_t, zero_s, wp, wv, wq, zp, zv, zq,
     ld_sem, own_sem, rv_send, rv_recv, re_send, re_recv, h_send, h_recv,
     m_send, m_recv, gm_send, gm_recv, c_send, c_recv, gc_send, gc_recv, ts_send, ts_recv,
 ):
@@ -23,14 +23,17 @@
     gz = lax.axis_index("gz")
     zi = gy // 8
     pi = gy % 8
-    xj = pi // 2
-    co = pi % 2
+    half = pi // 4
+    tile = pi % 4
 
     def to_y(k):
         return {"gz": (gz + k) % 8}
 
     def to_plane(k):
         return {"gy": zi * 8 + (pi + k) % 8}
+
+    def to_half(k):
+        return {"gy": zi * 8 + half * 4 + (tile + k) % 4}
 
     def to_z(k):
         return {"gy": ((zi + k) % 8) * 8 + pi}
@@ -44,6 +47,12 @@
             device_id=where, device_id_type=MESH,
         )
 
+    planes = [
+        pltpu.make_async_copy(vel, vs, ld_sem.at[5]),
+        pltpu.make_async_copy(exp, es, ld_sem.at[6]),
+    ]
+    for copy in planes:
+        copy.start()
     loads = []
     for h in range(2):
         loads.append(pltpu.make_async_copy(spk.at[:, pl.ds(h * 128, 128)], spk_h.at[h], ld_sem.at[h]))
@@ -52,12 +61,6 @@
     loads.append(pltpu.make_async_copy(bands_in, bands, ld_sem.at[4]))
     for copy in loads:
         copy.start()
-    mine = pl.ds(pl.multiple_of(gz * 512, 512), 512)
-    own_v = pltpu.make_async_copy(vel.at[:, :, mine], rv.at[gz], rv_recv.at[0])
-    own_e = pltpu.make_async_copy(exp.at[:, :, mine], re.at[gz], re_recv.at[0])
-    own_v.start()
-    own_e.start()
-
     barrier = pltpu.get_barrier_semaphore()
     for k in range(1, 8):
         for where in (to_y(k), to_z(k), to_plane(k)):
@@ -66,13 +69,19 @@
         pl.semaphore_signal(barrier, inc=1, device_id=to_next(k), device_id_type=MESH)
     pl.semaphore_wait(barrier, 23)
 
+    for copy in planes:
+        copy.wait()
     sends = []
-    for k in (4, 3, 5, 2, 6, 1, 7):
+    for k in (1, 7, 2, 6, 3, 5, 4):
         cols = pl.ds(pl.multiple_of(((gz + k) % 8) * 512, 512), 512)
-        for src, dst, send, recv in ((vel, rv, rv_send, rv_recv), (exp, re, re_send, re_recv)):
+        for src, dst, send, recv in ((vs, rv, rv_send, rv_recv), (es, re, re_send, re_recv)):
             copy = remote(src.at[:, :, cols], dst.at[gz], send.at[k], recv.at[k], to_y(k))
             copy.start()
             sends.append(copy)
+
+    mine = pl.ds(pl.multiple_of(gz * 512, 512), 512)
+    pltpu.make_async_copy(vs.at[:, :, mine], rv.at[gz], rv_recv.at[0]).start()
+    pltpu.make_async_copy(es.at[:, :, mine], re.at[gz], re_recv.at[0]).start()
 
     lane = lax.broadcasted_iota(jnp.int32, (24, 128), 1) // 2
     for h in range(2):
@@ -94,10 +103,10 @@
                 map_s[lt, i : i + 1, :] = -spk_d[lt, q * 24 + 22 + k : q * 24 + 23 + k, :]
                 map_s[lt, 4 + i : 5 + i, :] = -spk_d[lt, q * 24 + k : q * 24 + k + 1, :]
                 map_s[lt, 8 + i : 9 + i, :] = -spk_d[lt, 48 + q * 24 + k : 48 + q * 24 + k + 1, :]
-    map_r[pi] = map_s[xj]
+    map_r[pi] = map_s[tile]
     for k in range(1, 8):
         copy = remote(
-            map_s.at[(pi + k) % 8 // 2], map_r.at[pi], m_send.at[k], m_recv.at[k], to_plane(k)
+            map_s.at[(pi + k) % 4], map_r.at[pi], m_send.at[k], m_recv.at[k], to_plane(k)
         )
         copy.start()
         sends.append(copy)
@@ -110,6 +119,18 @@
         for i, row in ((d, first + second), (5 + d, first)):
             column = jnp.sum(jnp.where(eye, row, 0.0), axis=1, keepdims=True)
             coef[i] = jnp.broadcast_to(column, (24, 128))
+
+    for h in range(2):
+        loads[2 + h].wait()
+
+    def turn(c, carry):
+        for h in range(2):
+            part = inv_h[h, pl.ds(c, 24, stride=24), :]
+            for j in range(2):
+                inv_t[2 * h + j, c] = jnp.take_along_axis(part, lane + 64 * j, axis=1)
+        return carry
+
+    lax.fori_loop(0, 24, turn, 0)
 
     def apply2(maps, at, first, second):
         return (
@@ -150,6 +171,48 @@
         copy.start()
         sends.append(copy)
 
+    def weights(maps, hi, lo, p, v, q):
+        def times(x, m, at):
+            top, low = m[at : at + 2, :], m[at + 2 : at + 4, :]
+            return [row[0:1] * top + row[1:2] * low for row in x]
+
+        def put(where, x):
+            where[0:2] = x[0]
+            where[2:4] = x[1]
+
+        x = [jnp.zeros((2, 128), F32)] * 2
+        for g in range(8):
+            if g > 0:
+                x = times(x, maps[g - 1], 8)
+            x = [jnp.where(g == lo + 1, one, row) for one, row in zip(unit, x)]
+            put(q.at[g], x)
+        x = [jnp.zeros((2, 128), F32)] * 2
+        y = x
+        for g in range(7, -1, -1):
+            if g < 7:
+                m = maps[g + 1]
+                x = times(x, m, 0)
+                after = (q[g + 1, 0:2], q[g + 1, 2:4])
+                y = [a + b for a, b in zip(times(y, m, 0), times(after, m, 4))]
+            x = [jnp.where(g == hi - 1, one, row) for one, row in zip(unit, x)]
+            put(p.at[g], x)
+            put(v.at[g], y)
+
+    def gathered(p, v, q, got):
+        t = [jnp.zeros((3, 128), F32)] * 2
+        s = [jnp.zeros((3, 128), F32)] * 2
+        for g in range(8):
+            t_zero, t_one = got[g, 0:3, :], got[g, 3:6, :]
+            s_zero, s_one = got[g, 6:9, :], got[g, 9:12, :]
+            for k in range(2):
+                i = 2 * k
+                t[k] = t[k] + (p[g, i : i + 1] * t_zero + p[g, i + 1 : i + 2] * t_one)
+                s[k] = s[k] + (
+                    (v[g, i : i + 1] * t_zero + v[g, i + 1 : i + 2] * t_one)
+                    + (q[g, i : i + 1] * s_zero + q[g, i + 1 : i + 2] * s_one)
+                )
+        return t, s
+
     def wait_slot(slot):
         k = (gz - slot + 8) % 8
         pltpu.make_async_copy(rv.at[slot], rv.at[slot], rv_recv.at[k]).wait()
@@ -165,17 +228,7 @@
             sends.append(copy)
             halos.append(copy)
 
-    for h in range(2):
-        loads[2 + h].wait()
-
-    def turn(c, carry):
-        for h in range(2):
-            part = inv_h[h, pl.ds(c, 24, stride=24), :]
-            for j in range(2):
-                inv_t[2 * h + j, c] = jnp.take_along_axis(part, lane + 64 * j, axis=1)
-        return carry
-
-    lax.fori_loop(0, 24, turn, 0)
+    weights(map_r, 8, -1, wp, wv, wq)
 
     def gather_rows(g):
         def body(lt, carry):
@@ -228,23 +281,32 @@
 
     for k in range(1, 8):
         copy = remote(
-            cd_s.at[(pi + k) % 8 // 2], cd_r.at[pi], c_send.at[k], c_recv.at[k], to_plane(k)
+            cd_s.at[(pi + k) % 4], cd_r.at[pi], c_send.at[k], c_recv.at[k], to_plane(k)
         )
         copy.start()
         sends.append(copy)
-    cd_r[pi] = cd_s[xj]
+    cd_r[pi] = cd_s[tile]
     for k in range(1, 8):
         remote(gmap_s, gmap_r.at[(zi - k + 8) % 8], gm_send.at[k], gm_recv.at[k], to_z(k)).wait_recv()
+    weights(gmap_r, zi, zi, zp, zv, zq)
     for k in range(1, 8):
         remote(cd_s.at[0], cd_r.at[(pi - k + 8) % 8], c_send.at[k], c_recv.at[k], to_plane(k)).wait_recv()
+    t, s = gathered(wp, wv, wq, cd_r)
+    for k in range(2):
+        gcd_s[3 * k : 3 * k + 3] = t[k]
+        gcd_s[6 + 3 * k : 9 + 3 * k] = s[k]
+
+    for k in range(1, 8):
+        copy = remote(gcd_s, gcd_r.at[zi], gc_send.at[k], gc_recv.at[k], to_z(k))
+        copy.start()
+        sends.append(copy)
+    gcd_r[zi] = gcd_s[...]
     t0 = t1 = jnp.zeros((3, 128), F32)
     for b in range(8):
         zero_t[b, 0:3] = t0
         zero_t[b, 3:6] = t1
         n0, n1 = apply2(map_r[b], 0, t0, t1)
         t0, t1 = n0 + cd_r[b, 0:3, :], n1 + cd_r[b, 3:6, :]
-    gcd_s[0:3] = t0
-    gcd_s[3:6] = t1
     s0 = s1 = jnp.zeros((3, 128), F32)
     for b in range(7, -1, -1):
         zero_s[b, 0:3] = s0
@@ -252,32 +314,10 @@
         w0, w1 = apply2(map_r[b], 4, zero_t[b, 0:3], zero_t[b, 3:6])
         u0, u1 = apply2(map_r[b], 8, s0, s1)
         s0, s1 = u0 + (w0 + cd_r[b, 6:9, :]), u1 + (w1 + cd_r[b, 9:12, :])
-    gcd_s[6:9] = s0
-    gcd_s[9:12] = s1
-
-    for k in range(1, 8):
-        copy = remote(gcd_s, gcd_r.at[zi], gc_send.at[k], gc_recv.at[k], to_z(k))
-        copy.start()
-        sends.append(copy)
-    gcd_r[zi] = gcd_s[...]
     for k in range(1, 8):
         remote(gcd_s, gcd_r.at[(zi - k + 8) % 8], gc_send.at[k], gc_recv.at[k], to_z(k)).wait_recv()
-    t0 = t1 = jnp.zeros((3, 128), F32)
-    for g in range(8):
-        t_in[g, 0:3] = t0
-        t_in[g, 3:6] = t1
-        n0, n1 = apply2(gmap_r[g], 0, t0, t1)
-        t0, t1 = n0 + gcd_r[g, 0:3, :], n1 + gcd_r[g, 3:6, :]
-    s0 = s1 = jnp.zeros((3, 128), F32)
-    for g in range(7, -1, -1):
-        s_in[g, 0:3] = s0
-        s_in[g, 3:6] = s1
-        w0, w1 = apply2(gmap_r[g], 4, t_in[g, 0:3], t_in[g, 3:6])
-        u0, u1 = apply2(gmap_r[g], 8, s0, s1)
-        s0, s1 = u0 + (w0 + gcd_r[g, 6:9, :]), u1 + (w1 + gcd_r[g, 9:12, :])
-
-    t0, t1 = t_in[zi, 0:3], t_in[zi, 3:6]
-    s0, s1 = s_in[zi, 0:3], s_in[zi, 3:6]
+    (t0, t1), (s0, s1) = gathered(zp, zv, zq, gcd_r)
+
 
     def mapped(base, b, first, second):
         return (
@@ -286,7 +326,7 @@
         )
 
     for j in range(4):
-        b = 2 * j + co
+        b = 4 * half + j
         a0, a1 = mapped(base_t, b, t0, t1)
         ts_s[j, 0:3] = zero_t[b, 0:3] + a0
         ts_s[j, 3:6] = zero_t[b, 3:6] + a1
@@ -296,14 +336,14 @@
         ts_s[j, 9:12] = zero_s[b, 3:6] + a1 + b1
     for k in range(1, 4):
         copy = remote(
-            ts_s.at[(xj + k) % 4], ts_r.at[xj], ts_send.at[k], ts_recv.at[k], to_plane(2 * k)
+            ts_s.at[(tile + k) % 4], ts_r.at[tile], ts_send.at[k], ts_recv.at[k], to_half(k)
         )
         copy.start()
         sends.append(copy)
-    ts_r[xj] = ts_s[xj]
+    ts_r[tile] = ts_s[tile]
     for k in range(1, 4):
         remote(
-            ts_s.at[0], ts_r.at[(xj - k + 4) % 4], ts_send.at[k], ts_recv.at[k], to_plane(2 * k)
+            ts_s.at[0], ts_r.at[(tile - k + 4) % 4], ts_send.at[k], ts_recv.at[k], to_half(k)
         ).wait_recv()
 
     for lt in range(4):
@@ -332,7 +372,7 @@
         in_specs=[hbm] * 5,
         out_specs=pl.BlockSpec(memory_space=pltpu.VMEM),
         scratch_shapes=[
-            vmem(5, 2, 24),
+            vmem(5, 2, 24), vmem(3, 3, 4096), vmem(3, 3, 4096),
             vmem(8, 3, 3, 512), vmem(8, 3, 3, 512), vmem(2, 3, 3, 512), vmem(2, 3, 3, 512),
             vmem(2, 576, 128), vmem(4, 24, 24, 128), vmem(2, 96, 128), vmem(4, 96, 128),
             vmem(10, 24, 128), vmem(4, 3, 32, 128), vmem(4, 3, 32, 128),
@@ -341,8 +381,8 @@
             vmem(4, 12, 128), vmem(8, 12, 128), vmem(12, 128), vmem(8, 12, 128),
             vmem(8, 12, 128), vmem(4, 12, 128),
             vmem(8, 4, 128), vmem(8, 4, 128), vmem(8, 4, 128),
-            vmem(8, 6, 128), vmem(8, 6, 128), vmem(8, 6, 128), vmem(8, 6, 128),
-            dma((5,)), dma((2,)), dma((8,)), dma((8,)), dma((8,)), dma((8,)), dma((4,)), dma((4,)),
+            vmem(8, 6, 128), vmem(8, 6, 128), *[vmem(8, 4, 128) for _ in range(6)],
+            dma((7,)), dma((2,)), dma((8,)), dma((8,)), dma((8,)), dma((8,)), dma((4,)), dma((4,)),
             dma((8,)), dma((8,)), dma((8,)), dma((8,)), dma((8,)), dma((8,)), dma((8,)), dma((8,)),
             dma((4,)), dma((4,)),
         ],

time: 41 us -> 40.3 us (0.983)
  Pallas kernels: 40.3 us -> 39.5 us
    pallas_call x1, Pallas kernels: 40.3 us -> 39.5 us  [per_device(): pl.pallas_call(kernel, out_shape=jax.ShapeDtypeStruct((3, 24, 512), F32),...]
where the time goes in v3:
time: 40.3 us; the launch traced here: 40.2 us
  Pallas kernels  39.5 us (98%)
  local copies, waits for them, and re-layouts  0.66 us (2%)
    pallas_call x1, Pallas kernels, per_device(): pl.pallas_call(kernel, out_shape=jax.ShapeDtypeStruct((3, 24, 512), F32),...  39.5 us

profile of v3, /device:TPU:1, one launch (start us, length us, event | category | flops | bytes accessed | tf_op | source)
XLA Modules:
  0.0 40.2 jit_solution(6954994508396253835)
XLA Ops:
  0.0 39.5 %shard_map.55 = f32[3,24,512]{2,1,0:T(8,128)S(1)} custom-call(f32[3,3,4096]{2,1,0:T(4,128)} %vel.1, f32[3,3,4096]{2,1,0:T(4,128)} %exp.1, f32[5,2,24]{2,1,0:T(2,128)} %bitcast.5, f32[576,256]{1,0:T(8,128)} %bitcast.3, f32[96,256]{1,0:T(8,128)} %bitcast.4), custom_call_target="tpu_custom_call" | custom-call | tf_op jit(solution)/shard_map/pallas_call | solution.py:369
  39.5 0.7 %copy.7 = f32[3,24,512]{2,1,0:T(8,128)} copy(f32[3,24,512]{2,1,0:T(8,128)S(1)} %shard_map.55) | data formatting | bytes 294912

commit v4 on v3

--- a/solution.py
+++ b/solution.py
@@ -13,10 +13,10 @@
 
 def kernel(
     vel, exp, bands_in, inv, spk, out,
-    bands, vs, es, rv, re, hv, he, inv_h, inv_t, spk_h, spk_d, coef, vx, ex, rhs, local,
+    bands, own, got, edge, inv_h, inv_t, spk_h, spk_d, coef, vx, ex, rhs, local,
     map_s, map_r, gmap_s, gmap_r, cd_s, cd_r, gcd_s, gcd_r, ts_s, ts_r,
     base_t, base_s, base_r, zero_t, zero_s, wp, wv, wq, zp, zv, zq,
-    ld_sem, own_sem, rv_send, rv_recv, re_send, re_recv, h_send, h_recv,
+    ld_sem, got_send, got_recv, h_send, h_recv,
     m_send, m_recv, gm_send, gm_recv, c_send, c_recv, gc_send, gc_recv, ts_send, ts_recv,
 ):
     gy = lax.axis_index("gy")
@@ -47,9 +47,15 @@
             device_id=where, device_id_type=MESH,
         )
 
+    barrier = pltpu.get_barrier_semaphore()
+    for k in (4, 3, 5, 2, 6, 1, 7):
+        for where in (to_y(k), to_z(k), to_plane(k)):
+            pl.semaphore_signal(barrier, inc=1, device_id=where, device_id_type=MESH)
+    for k in (-1, 1):
+        pl.semaphore_signal(barrier, inc=1, device_id=to_next(k), device_id_type=MESH)
     planes = [
-        pltpu.make_async_copy(vel, vs, ld_sem.at[5]),
-        pltpu.make_async_copy(exp, es, ld_sem.at[6]),
+        pltpu.make_async_copy(vel, own.at[0], ld_sem.at[5]),
+        pltpu.make_async_copy(exp, own.at[1], ld_sem.at[6]),
     ]
     for copy in planes:
         copy.start()
@@ -61,12 +67,6 @@
     loads.append(pltpu.make_async_copy(bands_in, bands, ld_sem.at[4]))
     for copy in loads:
         copy.start()
-    barrier = pltpu.get_barrier_semaphore()
-    for k in range(1, 8):
-        for where in (to_y(k), to_z(k), to_plane(k)):
-            pl.semaphore_signal(barrier, inc=1, device_id=where, device_id_type=MESH)
-    for k in (-1, 1):
-        pl.semaphore_signal(barrier, inc=1, device_id=to_next(k), device_id_type=MESH)
     pl.semaphore_wait(barrier, 23)
 
     for copy in planes:
@@ -74,14 +74,11 @@
     sends = []
     for k in (1, 7, 2, 6, 3, 5, 4):
         cols = pl.ds(pl.multiple_of(((gz + k) % 8) * 512, 512), 512)
-        for src, dst, send, recv in ((vs, rv, rv_send, rv_recv), (es, re, re_send, re_recv)):
-            copy = remote(src.at[:, :, cols], dst.at[gz], send.at[k], recv.at[k], to_y(k))
-            copy.start()
-            sends.append(copy)
-
+        copy = remote(own.at[:, :, :, cols], got.at[gz], got_send.at[k], got_recv.at[k], to_y(k))
+        copy.start()
+        sends.append(copy)
     mine = pl.ds(pl.multiple_of(gz * 512, 512), 512)
-    pltpu.make_async_copy(vs.at[:, :, mine], rv.at[gz], rv_recv.at[0]).start()
-    pltpu.make_async_copy(es.at[:, :, mine], re.at[gz], re_recv.at[0]).start()
+    pltpu.make_async_copy(own.at[:, :, :, mine], got.at[gz], got_recv.at[0]).start()
 
     lane = lax.broadcasted_iota(jnp.int32, (24, 128), 1) // 2
     for h in range(2):
@@ -215,27 +212,24 @@
 
     def wait_slot(slot):
         k = (gz - slot + 8) % 8
-        pltpu.make_async_copy(rv.at[slot], rv.at[slot], rv_recv.at[k]).wait()
-        pltpu.make_async_copy(re.at[slot], re.at[slot], re_recv.at[k]).wait()
+        pltpu.make_async_copy(got.at[slot], got.at[slot], got_recv.at[k]).wait()
 
     halos = []
     for side, slot, step in ((0, 7, 1), (1, 0, -1)):
         wait_slot(slot)
-        for a, (src, dst) in enumerate(((rv, hv), (re, he))):
-            i = 2 * side + a
-            copy = remote(src.at[slot], dst.at[side], h_send.at[i], h_recv.at[i], to_next(step))
-            copy.start()
-            sends.append(copy)
-            halos.append(copy)
+        copy = remote(got.at[slot], edge.at[side], h_send.at[side], h_recv.at[side], to_next(step))
+        copy.start()
+        sends.append(copy)
+        halos.append(copy)
 
     weights(map_r, 8, -1, wp, wv, wq)
 
     def gather_rows(g):
         def body(lt, carry):
             cols = pl.ds(pl.multiple_of(lt * 128, 128), 128)
-            for got, rows in ((rv, vx), (re, ex)):
+            for a, rows in ((0, vx), (1, ex)):
                 for f in range(3):
-                    rows[lt, f, 2 + 3 * g : 5 + 3 * g, :] = got[g, f, :, cols]
+                    rows[lt, f, 2 + 3 * g : 5 + 3 * g, :] = got[g, a, f, :, cols]
             return carry
 
         lax.fori_loop(0, 4, body, 0)
@@ -250,10 +244,10 @@
 
     def gather_edges(lt, carry):
         cols = pl.ds(pl.multiple_of(lt * 128, 128), 128)
-        for got, rows in ((hv, vx), (he, ex)):
+        for a, rows in ((0, vx), (1, ex)):
             for f in range(3):
-                rows[lt, f, 0:2, :] = jnp.where(gy > 0, got[0, f, 1:3, cols], 0.0)
-                rows[lt, f, 26:28, :] = jnp.where(gy < 63, got[1, f, 0:2, cols], 0.0)
+                rows[lt, f, 0:2, :] = jnp.where(gy > 0, edge[0, a, f, 1:3, cols], 0.0)
+                rows[lt, f, 26:28, :] = jnp.where(gy < 63, edge[1, a, f, 0:2, cols], 0.0)
         return carry
 
     lax.fori_loop(0, 4, gather_edges, 0)
@@ -372,8 +366,8 @@
         in_specs=[hbm] * 5,
         out_specs=pl.BlockSpec(memory_space=pltpu.VMEM),
         scratch_shapes=[
-            vmem(5, 2, 24), vmem(3, 3, 4096), vmem(3, 3, 4096),
-            vmem(8, 3, 3, 512), vmem(8, 3, 3, 512), vmem(2, 3, 3, 512), vmem(2, 3, 3, 512),
+            vmem(5, 2, 24), vmem(2, 3, 3, 4096),
+            vmem(8, 2, 3, 3, 512), vmem(2, 2, 3, 3, 512),
             vmem(2, 576, 128), vmem(4, 24, 24, 128), vmem(2, 96, 128), vmem(4, 96, 128),
             vmem(10, 24, 128), vmem(4, 3, 32, 128), vmem(4, 3, 32, 128),
             vmem(4, 3, 24, 128), vmem(4, 3, 24, 128),
@@ -382,7 +376,7 @@
             vmem(8, 12, 128), vmem(4, 12, 128),
             vmem(8, 4, 128), vmem(8, 4, 128), vmem(8, 4, 128),
             vmem(8, 6, 128), vmem(8, 6, 128), *[vmem(8, 4, 128) for _ in range(6)],
-            dma((7,)), dma((2,)), dma((8,)), dma((8,)), dma((8,)), dma((8,)), dma((4,)), dma((4,)),
+            dma((7,)), dma((8,)), dma((8,)), dma((2,)), dma((2,)),
             dma((8,)), dma((8,)), dma((8,)), dma((8,)), dma((8,)), dma((8,)), dma((8,)), dma((8,)),
             dma((4,)), dma((4,)),
         ],

time: 40.3 us -> 39.9 us (0.990)
  no operation moved by 1% of the time
where the time goes in v4:
time: 39.9 us; the launch traced here: 39.8 us
  Pallas kernels  39.2 us (98%)
  local copies, waits for them, and re-layouts  0.66 us (2%)
    pallas_call x1, Pallas kernels, per_device(): pl.pallas_call(kernel, out_shape=jax.ShapeDtypeStruct((3, 24, 512), F32),...  39.2 us

profile of v4, /device:TPU:1, one launch (start us, length us, event | category | flops | bytes accessed | tf_op | source)
XLA Modules:
  0.0 39.8 jit_solution(14700689483351773266)
XLA Ops:
  0.0 39.2 %shard_map.55 = f32[3,24,512]{2,1,0:T(8,128)S(1)} custom-call(f32[3,3,4096]{2,1,0:T(4,128)} %vel.1, f32[3,3,4096]{2,1,0:T(4,128)} %exp.1, f32[5,2,24]{2,1,0:T(2,128)} %bitcast.5, f32[576,256]{1,0:T(8,128)} %bitcast.3, f32[96,256]{1,0:T(8,128)} %bitcast.4), custom_call_target="tpu_custom_call" | custom-call | tf_op jit(solution)/shard_map/pallas_call | solution.py:363
  39.2 0.7 %copy.7 = f32[3,24,512]{2,1,0:T(8,128)} copy(f32[3,24,512]{2,1,0:T(8,128)S(1)} %shard_map.55) | data formatting | bytes 294912
